TPU v7x, 256 devices: a whole 4x4x8 slice. The times are simulated.
256 devices in a mesh: tm: 4 (over x), rows: 64 (over y, z, core).
Axes of the slice: x: 4, y: 4, z: 8, core: 2. Of those that a mesh axis runs over, the one named last changes fastest.
Arguments:
- latent: bfloat16 [4, 64, 160, 512], P('tm', 'rows'), may hold values from -350 to 350, as said below
- norm_gain: float32 [512], replicated, may hold values from 0.1 to 1.9
- norm_bias: float32 [512], replicated, may hold values from -4 to 4
- conv_weight: bfloat16 [3, 3, 3, 512, 512], P(None, None, None, 'rows', 'tm'), may hold values from -0.0546875 to 0.0546875
- cotangent: bfloat16 [4, 128, 320, 512], P('tm', 'rows'), may hold values from -180 to 180
Outputs:
- latent_grad: float32 [4, 64, 160, 512], P('tm', 'rows')
- gain_grad: float32 [512], replicated
- bias_grad: float32 [512], replicated
Inputs may be any that keep to these rules, and one draw needn't show every extreme that they name: `latent`: features of the unit's input.
All inputs are finite; a program needn't handle non-finite values.
Results may differ from a plain program's by a relative error of at most 0.0003.
Values may be sent and summed in bfloat16 or wider, within the bound.
No kernel may reach another device: no remote copies, remote signals or barrier semaphores. Data moves between devices by JAX's collectives and lax.ppermute only.
A program may use at most 320 MiB of HBM per device.

v0:
```python
import jax
import jax.numpy as jnp
from jax import lax
from jax.sharding import PartitionSpec as P

GROUPS = 32


def extended(block, sides, width):
    for axis, dim in sides:
        count = lax.axis_size(axis)
        forward = [(i, i + 1) for i in range(count - 1)]
        backward = [(target, source) for source, target in forward]
        low = lax.ppermute(
            lax.slice_in_dim(block, block.shape[dim] - width, None, axis=dim), axis, forward
        )
        high = lax.ppermute(lax.slice_in_dim(block, 0, width, axis=dim), axis, backward)
        block = jnp.concatenate([low, block, high], axis=dim)
    return block


def from_behind(value, axis, steps):
    count = lax.axis_size(axis)
    first, last = (max(0, -steps), min(count, count - steps))
    return lax.ppermute(value, axis, [(source, source + steps) for source in range(first, last)])


def shifted_rows(frames, extra_frames):
    padded = jnp.pad(frames, ((0, extra_frames), (0, 0), (1, 1), (0, 0)))
    fine_rows = frames.shape[1] - 2
    return [padded[:, 2 - row_tap : 2 - row_tap + fine_rows] for row_tap in range(3)]


def tap_total(row_slabs, weights, tap_pairs, frames_out, span_cols):
    running = None
    for offset, tap_index in tap_pairs:
        for row_tap in range(3):
            source = row_slabs[row_tap][offset : offset + frames_out]
            for col_tap in range(3):
                product = lax.dot_general(
                    source,
                    weights[tap_index, row_tap, col_tap],
                    (((3,), (1,)), ((), ())),
                    preferred_element_type=jnp.float32,
                )
                piece = product[:, :, 2 - col_tap : 2 - col_tap + span_cols, :]
                running = piece if running is None else running + piece
    return running


def pool_pairs(fine_grad):
    frames, fine_rows, span_cols, channels = fine_grad.shape
    return fine_grad.reshape(frames, fine_rows // 2, 2, span_cols // 2, 2, channels).sum(
        axis=(2, 4)
    )


def block_grad(row_slabs, weights, frames_out, first_frame):
    span_cols = row_slabs[0].shape[2] - 2

    def extra_terms():
        return tap_total(row_slabs, weights, ((0, 1), (0, 0), (1, 0)), 1, span_cols)

    def no_terms():
        return jnp.zeros((1, row_slabs[0].shape[1], span_cols, weights.shape[3]), jnp.float32)

    main_part = tap_total(row_slabs, weights, ((0, 2), (1, 1), (2, 0)), frames_out, span_cols)
    main_part = main_part + lax.cond(first_frame, extra_terms, no_terms)
    return pool_pairs(main_part)


def on_device(latent, norm_gain, norm_bias, conv_weight, cotangent):
    frames_all = lax.axis_size("tm")
    rows_all = lax.axis_size("rows")
    low_rows = latent.shape[1]
    low_cols = latent.shape[2]
    channels = latent.shape[3]
    per_group = channels // GROUPS
    cell_count = frames_all * rows_all * low_rows * low_cols
    rimmed = extended(cotangent, (("rows", 1),), 1)
    following = from_behind(rimmed, "tm", -1)
    further = from_behind(rimmed, "tm", -2)
    stacked = jnp.concatenate([rimmed, following, further], axis=0)
    weight_wide = lax.all_gather(conv_weight, "tm", axis=4, tiled=True)
    weight_full = lax.all_gather(weight_wide, "rows", axis=3, tiled=True)
    up_grad = block_grad(shifted_rows(stacked, 0), weight_full, 1, lax.axis_index("tm") == 0)
    features = latent.astype(jnp.float32)
    sum_x = jnp.sum(features, axis=(0, 1, 2))
    sum_sq = jnp.sum(features * features, axis=(0, 1, 2))
    total_x, total_sq = lax.psum((sum_x, sum_sq), ("tm", "rows"))
    group_x = total_x.reshape(GROUPS, per_group).sum(axis=1)
    group_sq = total_sq.reshape(GROUPS, per_group).sum(axis=1)
    group_mean = group_x / (cell_count * per_group)
    group_var = group_sq / (cell_count * per_group) - group_mean * group_mean
    inv_std = lax.rsqrt(group_var + 1e-06)
    mean_chan = jnp.repeat(group_mean, per_group)
    inv_chan = jnp.repeat(inv_std, per_group)
    normed = (features - mean_chan) * inv_chan
    pre = normed * norm_gain + norm_bias
    sigmoid_pre = jax.nn.sigmoid(pre)
    act_grad = up_grad * sigmoid_pre * (1.0 + pre * (1.0 - sigmoid_pre))
    sum_act, sum_scaled = lax.psum(
        (jnp.sum(act_grad, axis=(0, 1, 2)), jnp.sum(act_grad * normed, axis=(0, 1, 2))),
        ("tm", "rows"),
    )
    gain_grad = sum_scaled / cell_count
    bias_grad = sum_act / cell_count
    mean_q = (norm_gain * sum_act).reshape(GROUPS, per_group).sum(axis=1) / (cell_count * per_group)
    mean_qn = (norm_gain * sum_scaled).reshape(GROUPS, per_group).sum(axis=1) / (
        cell_count * per_group
    )
    latent_grad = inv_chan * (
        act_grad * norm_gain
        - jnp.repeat(mean_q, per_group)
        - normed * jnp.repeat(mean_qn, per_group)
    )
    return (latent_grad, gain_grad, bias_grad)


def solution(mesh):
    placed = (
        P("tm", "rows", None, None),
        P(),
        P(),
        P(None, None, None, "rows", "tm"),
        P("tm", "rows", None, None),
    )
    return jax.shard_map(
        on_device,
        mesh=mesh,
        in_specs=placed,
        out_specs=(P("tm", "rows", None, None), P(), P()),
        check_vma=False,
    )
```

profile of v0, /device:TPU:1, one launch (start us, length us, event | category | flops | bytes accessed | tf_op | source)
XLA Modules:
  0.0 354.6 jit_solution(4041163253013684087)
XLA Ops:
  7.2 11.7 %all_gather.6 = bf16[3,3,3,8,512]{4,3,2,1,0:T(8,128)(2,1)} all-gather(bf16[3,3,3,8,128]{4,3,2,1,0:T(8,128)(2,1)} %param.10), channel_id=1, replica_groups=mesh['tm'=4,'rows'=64] {'tm'}, dimensions={4}, use_global_device_ids=true | all-gather | bytes 276480 | tf_op jit(solution)/shard_map/all_gather | solution.py:84
  20.1 6.2 %collective-permute-start = (bf16[1,1,320,512]{3,2,1,0:T(8,128)(2,1)S(1)}, bf16[1,1,320,512]{3,2,1,0:T(8,128)(2,1)S(1)}, u32[]{:S(2)}, u32[]{:S(2)}) collective-permute-start(bf16[1,1,320,512]{3,2,1,0:T(8,128)(2,1)S(1)} %get-tuple-element.27), channel_id=1, source_target_pairs={{0,1},{1,2},{2,3},{3,4},{4,5},{5,6},{6,7},{7,8},{8,9},{9,10},{10,1... | collective-permute-start | bytes 983048 | tf_op jit(solution)/shard_map/ppermute | solution.py:14
  26.3 1.9 collective-permute-start.1
  28.2 2.1 collective-permute-done
  30.4 4.3 %collective-permute-done.1 = bf16[1,1,320,512]{3,2,1,0:T(8,128)(2,1)S(1)} collective-permute-done((bf16[1,1,320,512]{3,2,1,0:T(8,128)(2,1)S(1)}, bf16[1,1,320,512]{3,2,1,0:T(8,128)(2,1)S(1)}, u32[]{:S(2)}, u32[]{:S(2)}) %collective-permute-start.1) | collective-permute-done | bytes 327712 | tf_op jit(solution)/shard_map/ppermute | solution.py:17
  37.6 129.7 %all-reduce.2 = (f32[32,16]{1,0:T(8,128)S(1)}, f32[32,16]{1,0:T(8,128)S(1)}) all-reduce(f32[32,16]{1,0:T(8,128)S(1)} %reshape.178, f32[32,16]{1,0:T(8,128)S(1)} %reshape.177), channel_id=1, replica_groups=mesh['tm'=4,'rows'=64] {'tm','rows'}, use_global_device_ids=true, to_apply=%region_4.5 | all-reduce | flops 1024 | bytes 8192 | tf_op jit(solution)/shard_map/psum | solution.py:90
  167.8 3.9 %fusion.113 = bf16[3,4,322,512]{3,2,1,0:T(8,128)(2,1)} fusion(bf16[1,4,320,512]{3,2,1,0:T(8,128)(2,1)} %collective-permute-done.3, bf16[1,4,320,512]{3,2,1,0:T(8,128)(2,1)} %collective-permute-done.2, bf16[1,4,320,512]{3,2,1,0:T(8,128)(2,1)S(1)} %constant_dynamic-update-slice_fusion), kind=kLoop, calls=%fused_computation.168 | loop fusion | flops 23740416 | bytes 7888896 | tf_op jit(solution)/shard_map/concatenate | solution.py:83
  171.7 48.1 %conditional.1 = (f32[1,2,320,512]{3,2,1,0:T(8,128)}) conditional(s32[]{:T(128)} %convert_element_type.9, () %tuple.14, (bf16[3,4,322,512]{3,2,1,0:T(8,128)(2,1)}, bf16[3,3,3,512,512]{4,3,2,1,0:T(8,128)(2,1)}) %tuple.15), branch_computations={%region_6.7_spmd, %region_7.8_spmd} | conditional | flops 9124839424 | bytes 177053760 | solution.py:68
  171.7 1.9 convolution_bitcast_fusion.15
  173.6 1.8 convolution_bitcast_fusion.16
  175.5 1.7 convolution_bitcast_fusion.17
  177.2 2.0 convolution_bitcast_fusion.24
  179.2 2.1 convolution_bitcast_fusion.25
  189.4 1.6 convolution_bitcast_fusion.19
  191.0 1.6 convolution_bitcast_fusion.6
  192.7 1.6 convolution_bitcast_fusion.7
  194.3 1.7 convolution_bitcast_fusion.3
  195.9 1.6 convolution_bitcast_fusion.4
  197.5 1.6 convolution_bitcast_fusion
  199.2 1.6 convolution_bitcast_fusion.1
  200.8 1.6 convolution_bitcast_fusion.2
  202.4 1.7 convolution_bitcast_fusion.5
  204.1 1.7 convolution_bitcast_fusion.8
  205.8 1.7 convolution_bitcast_fusion.20
  207.5 1.6 convolution_bitcast_fusion.23
  209.1 1.6 convolution_bitcast_fusion.26
  210.7 9.0 %slice_add_fusion = f32[1,2,320,512]{3,2,1,0:T(8,128)} fusion(f32[1,2,322,512]{3,2,1,0:T(8,128)} %convolution_bitcast_fusion, f32[1,2,322,512]{3,2,1,0:T(8,128)} %convolution_bitcast_fusion.1, f32[1,2,322,512]{3,2,1,0:T(8,128)} %convolution_bitcast_fusion.2, f32[1,2,322,512]{3,2,1,0:T(8,128)} %convolution_bitcast_fusion.3, ...), kind=kLoop, calls=%fused_computation.27 | loop fusion | flops 8519680 | bytes 36700160 | tf_op jit(solution)/shard_map/cond/branch_1_fun/add | solution.py:47
  219.8 1.9 convolution_bitcast_fusion.28
  221.7 1.8 convolution_bitcast_fusion.27
  223.6 1.7 convolution_bitcast_fusion.31
  225.3 2.0 convolution_bitcast_fusion.30
  227.3 2.1 convolution_bitcast_fusion.34
  237.0 1.7 convolution_bitcast_fusion.45
  238.7 1.7 convolution_bitcast_fusion.49
  240.4 1.6 convolution_bitcast_fusion.48
  242.0 1.6 convolution_bitcast_fusion.52
  243.6 1.6 convolution_bitcast_fusion.51
  245.2 1.6 convolution_bitcast_fusion.29
  246.9 1.6 convolution_bitcast_fusion.32
  248.5 1.6 convolution_bitcast_fusion.35
  250.1 1.6 convolution_bitcast_fusion.38
  251.7 1.7 convolution_bitcast_fusion.41
  253.4 1.6 convolution_bitcast_fusion.44
  255.0 1.6 convolution_bitcast_fusion.47
  256.6 1.6 convolution_bitcast_fusion.50
  258.2 1.7 convolution_bitcast_fusion.53
  259.9 10.1 %fusion.115 = f32[320,512]{1,0:T(8,128)} fusion(f32[1,2,320,512]{3,2,1,0:T(8,128)} %get-tuple-element.34, f32[1,2,322,512]{3,2,1,0:T(8,128)S(1)} %convolution_bitcast_fusion.27, f32[1,2,322,512]{3,2,1,0:T(8,128)S(1)} %convolution_bitcast_fusion.28, f32[1,2,322,512]{3,2,1,0:T(8,128)} %convolution_bitcast_fusion.29, ...), kind=kLoop, calls=%fused_computation.198 | loop fusion | flops 9011200 | bytes 37355520 | tf_op jit(solution)/shard_map/reduce_sum | solution.py:53
  272.5 73.1 %all-reduce.1 = (f32[512]{0:T(512)S(1)}, f32[512]{0:T(512)S(1)}) all-reduce(f32[512]{0:T(512)S(1)} %get-tuple-element.18, f32[512]{0:T(512)S(1)} %get-tuple-element.17), channel_id=1, replica_groups=mesh['tm'=4,'rows'=64] {'tm','rows'}, use_global_device_ids=true, to_apply=%region_14.15 | all-reduce | flops 1024 | bytes 8192 | tf_op jit(solution)/shard_map/psum | solution.py:102
  (69 shorter events, 24.7 us)
Async XLA Ops:
  7.2 23.2 %copy-start.4 = (bf16[1,2,320,512]{3,2,1,0:T(8,128)(2,1)S(1)}, bf16[1,2,320,512]{3,2,1,0:T(8,128)(2,1)}, u32[]{:S(2)}) copy-start(bf16[1,2,320,512]{3,2,1,0:T(8,128)(2,1)} %param.11) | copy-start | bytes 1966084
  7.2 164.5 %all-gather.2.cloned.1.call-start = ((), (), s32[]{:S(2)}) async-start(), calls=%async_computation | async-start | bytes 14376960 | tf_op jit(solution)/shard_map/all_gather | solution.py:85
  20.0 17.3 %copy-start.5 = (bf16[1,1,160,512]{3,2,1,0:T(8,128)(2,1)S(1)}, bf16[1,1,160,512]{3,2,1,0:T(8,128)(2,1)}, u32[]{:S(2)}) copy-start(bf16[1,1,160,512]{3,2,1,0:T(8,128)(2,1)} %param.7) | copy-start | bytes 491524
  20.1 10.2 %collective-permute-start = (bf16[1,1,320,512]{3,2,1,0:T(8,128)(2,1)S(1)}, bf16[1,1,320,512]{3,2,1,0:T(8,128)(2,1)S(1)}, u32[]{:S(2)}, u32[]{:S(2)}) collective-permute-start(bf16[1,1,320,512]{3,2,1,0:T(8,128)(2,1)S(1)} %get-tuple-element.27), channel_id=1, source_target_pairs={{0,1},{1,2},{2,3},{3,4},{4,5},{5,6},{6,7},{7,8},{8,9},{9,10},{10,1... | collective-permute-start | bytes 983048 | tf_op jit(solution)/shard_map/ppermute | solution.py:14
  26.3 8.4 %collective-permute-start.1 = (bf16[1,1,320,512]{3,2,1,0:T(8,128)(2,1)S(1)}, bf16[1,1,320,512]{3,2,1,0:T(8,128)(2,1)S(1)}, u32[]{:S(2)}, u32[]{:S(2)}) collective-permute-start(bf16[1,1,320,512]{3,2,1,0:T(8,128)(2,1)S(1)} %get-tuple-element.26), channel_id=1, source_target_pairs={{1,0},{2,1},{3,2},{4,3},{5,4},{6,5},{7,6},{8,7},{9,8},{10,9},{11,1... | collective-permute-start | bytes 983048 | tf_op jit(solution)/shard_map/ppermute | solution.py:17
  34.7 133.1 %collective-permute-start.3 = (bf16[1,4,320,512]{3,2,1,0:T(8,128)(2,1)S(1)}, bf16[1,4,320,512]{3,2,1,0:T(8,128)(2,1)}, u32[]{:S(2)}, u32[]{:S(2)}) collective-permute-start(bf16[1,4,320,512]{3,2,1,0:T(8,128)(2,1)S(1)} %constant_dynamic-update-slice_fusion), channel_id=1, source_target_pairs={{128,0},{192,64},{129,1},{193,65},{130,2},{194,66},{131,3},{195,67... | collective-permute-start | bytes 3932168 | tf_op jit(solution)/shard_map/ppermute | solution.py:25
  36.0 131.8 %collective-permute-start.2 = (bf16[1,4,320,512]{3,2,1,0:T(8,128)(2,1)S(1)}, bf16[1,4,320,512]{3,2,1,0:T(8,128)(2,1)}, u32[]{:S(2)}, u32[]{:S(2)}) collective-permute-start(bf16[1,4,320,512]{3,2,1,0:T(8,128)(2,1)S(1)} %constant_dynamic-update-slice_fusion), channel_id=1, source_target_pairs={{64,0},{128,64},{192,128},{65,1},{129,65},{193,129},{66,2},{130,66... | collective-permute-start | bytes 3932168 | tf_op jit(solution)/shard_map/ppermute | solution.py:25
  171.7 3.7 %copy-start.1 = (bf16[3,4,322,512]{3,2,1,0:T(8,128)(2,1)S(1)}, bf16[3,4,322,512]{3,2,1,0:T(8,128)(2,1)}, u32[]{:S(2)}) copy-start(bf16[3,4,322,512]{3,2,1,0:T(8,128)(2,1)} %get-tuple-element.12) | copy-start | bytes 11870212 | tf_op jit(solution)/shard_map/cond
  175.4 10.7 %copy-start.3 = (bf16[3,3,3,512,512]{4,3,2,1,0:T(8,128)(2,1)S(1)}, bf16[3,3,3,512,512]{4,3,2,1,0:T(8,128)(2,1)}, u32[]{:S(2)}) copy-start(bf16[3,3,3,512,512]{4,3,2,1,0:T(8,128)(2,1)} %get-tuple-element.13) | copy-start | bytes 42467332 | tf_op jit(solution)/shard_map/cond
  219.8 3.7 %copy-start = (bf16[3,4,322,512]{3,2,1,0:T(8,128)(2,1)S(1)}, bf16[3,4,322,512]{3,2,1,0:T(8,128)(2,1)}, u32[]{:S(2)}) copy-start(bf16[3,4,322,512]{3,2,1,0:T(8,128)(2,1)} %fusion.113) | copy-start | bytes 11870212
  223.5 10.7 %copy-start.2 = (bf16[3,3,3,512,512]{4,3,2,1,0:T(8,128)(2,1)S(1)}, bf16[3,3,3,512,512]{4,3,2,1,0:T(8,128)(2,1)}, u32[]{:S(2)}) copy-start(bf16[3,3,3,512,512]{4,3,2,1,0:T(8,128)(2,1)} %all-gather.2.cloned.1.call-done) | copy-start | bytes 42467332
  270.0 2.3 copy-start.6
  270.0 2.3 copy-start.7
Sparse Core Ops, SparseCore 0:
  19.0 105.3 all-gather.1
where the time goes:
time: 355 us
  blocking collectives  214 us (60%)
  matrix products  78.8 us (22%)
  other arithmetic  26 us (7%)
  between operations  14.3 us (4%)
  starting transfers between devices  10.8 us (3%)
  waiting for transfers between devices  6.41 us (2%)
  local copies, waits for them, and re-layouts  3.66 us (1%)
    psum x1, blocking collectives, on_device(): total_x, total_sq = lax.psum((sum_x, sum_sq), ('tm', 'rows'))  130 us
    dot_general x54, matrix products, tap_total(): lax.dot_general(source, weights[tap_index, row_tap, col_tap], (((3,), (1,...  78.8 us
    psum x1, blocking collectives, on_device(): lax.psum((jnp.sum(act_grad, axis=(0, 1, 2)), jnp.sum(act_grad * normed, a...  73.1 us
    all_gather x1, blocking collectives, on_device(): weight_wide = lax.all_gather(conv_weight, 'tm', axis=4, tiled=True)  11.7 us
    reduce_sum x2, other arithmetic, pool_pairs(): fine_grad.reshape(frames, fine_rows // 2, 2, span_cols // 2, 2, channels)  10.9 us
    add x1, other arithmetic, tap_total(): running = piece if running is None else running + piece  9.05 us
  transfers between devices with their start and end apart: 5, of which 2 were waited for; matrix products, arithmetic and copies ran while one was open for 2% of the time, Pallas kernels for 0%

commit v1 on v0

--- a/solution.py
+++ b/solution.py
@@ -1,9 +1,19 @@
+import functools
 import jax
 import jax.numpy as jnp
 from jax import lax
 from jax.sharding import PartitionSpec as P
 
 GROUPS = 32
+
+
+def draw_links(block_here, row_axis, named_axis):
+    for rr in (row_axis, named_axis):
+        block_here = lax.psum(block_here, rr)
+    return block_here
+
+
+form_page = functools.partial(draw_links, row_axis="tm", named_axis="rows")
 
 
 def extended(block, sides, width):
@@ -99,9 +109,8 @@
     pre = normed * norm_gain + norm_bias
     sigmoid_pre = jax.nn.sigmoid(pre)
     act_grad = up_grad * sigmoid_pre * (1.0 + pre * (1.0 - sigmoid_pre))
-    sum_act, sum_scaled = lax.psum(
-        (jnp.sum(act_grad, axis=(0, 1, 2)), jnp.sum(act_grad * normed, axis=(0, 1, 2))),
-        ("tm", "rows"),
+    sum_act, sum_scaled = form_page(
+        (jnp.sum(act_grad, axis=(0, 1, 2)), jnp.sum(act_grad * normed, axis=(0, 1, 2)))
     )
     gain_grad = sum_scaled / cell_count
     bias_grad = sum_act / cell_count

time: 355 us -> 414 us (1.17)
  blocking collectives: 214 us -> 273 us
    psum x1 -> x2, blocking collectives: 73.1 us -> 132 us  [draw_links(): block_here = lax.psum(block_here, rr)]
  transfers between devices with their start and end apart: 5 -> 5, of which waited for: 2 -> 2; matrix products, arithmetic and copies ran while one was open for 2% -> 1% of each run, Pallas kernels for 0% -> 0%
where the time goes in v1:
time: 414 us; the launch traced here: 413 us
  blocking collectives  273 us (66%)
  matrix products  78.8 us (19%)
  other arithmetic  26 us (6%)
  between operations  14.3 us (3%)
  starting transfers between devices  10.8 us (3%)
  waiting for transfers between devices  6.41 us (2%)
    psum x2, blocking collectives, draw_links(): block_here = lax.psum(block_here, rr)  132 us
    psum x1, blocking collectives, on_device(): total_x, total_sq = lax.psum((sum_x, sum_sq), ('tm', 'rows'))  130 us
    dot_general x54, matrix products, tap_total(): lax.dot_general(source, weights[tap_index, row_tap, col_tap], (((3,), (1,...  78.8 us
    all_gather x1, blocking collectives, on_device(): weight_wide = lax.all_gather(conv_weight, 'tm', axis=4, tiled=True)  11.7 us
    reduce_sum x2, other arithmetic, pool_pairs(): fine_grad.reshape(frames, fine_rows // 2, 2, span_cols // 2, 2, channels)  10.9 us
    add x1, other arithmetic, tap_total(): running = piece if running is None else running + piece  9.05 us
  transfers between devices with their start and end apart: 5, of which 2 were waited for; matrix products, arithmetic and copies ran while one was open for 1% of the time, Pallas kernels for 0%

profile of v1, /device:TPU:1, one launch (start us, length us, event | category | flops | bytes accessed | tf_op | source)
XLA Modules:
  0.0 413.3 jit_solution(13539322158960216465)
XLA Ops:
  7.2 11.7 %all_gather.6 = bf16[3,3,3,8,512]{4,3,2,1,0:T(8,128)(2,1)} all-gather(bf16[3,3,3,8,128]{4,3,2,1,0:T(8,128)(2,1)} %param.10), channel_id=1, replica_groups=mesh['tm'=4,'rows'=64] {'tm'}, dimensions={4}, use_global_device_ids=true | all-gather | bytes 276480 | tf_op jit(solution)/shard_map/all_gather | solution.py:94
  20.1 6.2 %collective-permute-start = (bf16[1,1,320,512]{3,2,1,0:T(8,128)(2,1)S(1)}, bf16[1,1,320,512]{3,2,1,0:T(8,128)(2,1)S(1)}, u32[]{:S(2)}, u32[]{:S(2)}) collective-permute-start(bf16[1,1,320,512]{3,2,1,0:T(8,128)(2,1)S(1)} %get-tuple-element.29), channel_id=1, source_target_pairs={{0,1},{1,2},{2,3},{3,4},{4,5},{5,6},{6,7},{7,8},{8,9},{9,10},{10,1... | collective-permute-start | bytes 983048 | tf_op jit(solution)/shard_map/ppermute | solution.py:24
  26.3 1.9 collective-permute-start.1
  28.2 2.1 collective-permute-done
  30.4 4.3 %collective-permute-done.1 = bf16[1,1,320,512]{3,2,1,0:T(8,128)(2,1)S(1)} collective-permute-done((bf16[1,1,320,512]{3,2,1,0:T(8,128)(2,1)S(1)}, bf16[1,1,320,512]{3,2,1,0:T(8,128)(2,1)S(1)}, u32[]{:S(2)}, u32[]{:S(2)}) %collective-permute-start.1) | collective-permute-done | bytes 327712 | tf_op jit(solution)/shard_map/ppermute | solution.py:27
  37.6 129.7 %all-reduce.1 = (f32[32,16]{1,0:T(8,128)S(1)}, f32[32,16]{1,0:T(8,128)S(1)}) all-reduce(f32[32,16]{1,0:T(8,128)S(1)} %reshape.178, f32[32,16]{1,0:T(8,128)S(1)} %reshape.177), channel_id=1, replica_groups=mesh['tm'=4,'rows'=64] {'tm','rows'}, use_global_device_ids=true, to_apply=%region_4.5 | all-reduce | flops 1024 | bytes 8192 | tf_op jit(solution)/shard_map/psum | solution.py:100
  167.8 3.9 fusion.113
  171.7 48.1 %conditional.1 = (f32[1,2,320,512]{3,2,1,0:T(8,128)}) conditional(s32[]{:T(128)} %convert_element_type.9, () %tuple.14, (bf16[3,4,322,512]{3,2,1,0:T(8,128)(2,1)}, bf16[3,3,3,512,512]{4,3,2,1,0:T(8,128)(2,1)}) %tuple.15), branch_computations={%region_6.7_spmd, %region_7.8_spmd} | conditional | flops 9124839424 | bytes 177053760 | solution.py:78
  171.7 1.9 convolution_bitcast_fusion.15
  173.7 1.8 convolution_bitcast_fusion.16
  175.5 1.7 convolution_bitcast_fusion.17
  177.2 2.0 convolution_bitcast_fusion.24
  179.2 2.1 convolution_bitcast_fusion.25
  189.4 1.6 convolution_bitcast_fusion.19
  191.1 1.6 convolution_bitcast_fusion.6
  192.7 1.6 convolution_bitcast_fusion.7
  194.3 1.7 convolution_bitcast_fusion.3
  196.0 1.6 convolution_bitcast_fusion.4
  197.6 1.6 convolution_bitcast_fusion
  199.2 1.6 convolution_bitcast_fusion.1
  202.4 1.7 convolution_bitcast_fusion.5
  204.1 1.7 convolution_bitcast_fusion.8
  205.8 1.7 convolution_bitcast_fusion.20
  207.5 1.6 convolution_bitcast_fusion.23
  209.1 1.6 convolution_bitcast_fusion.26
  210.8 9.0 %slice_add_fusion = f32[1,2,320,512]{3,2,1,0:T(8,128)} fusion(f32[1,2,322,512]{3,2,1,0:T(8,128)} %convolution_bitcast_fusion, f32[1,2,322,512]{3,2,1,0:T(8,128)} %convolution_bitcast_fusion.1, f32[1,2,322,512]{3,2,1,0:T(8,128)} %convolution_bitcast_fusion.2, f32[1,2,322,512]{3,2,1,0:T(8,128)} %convolution_bitcast_fusion.3, ...), kind=kLoop, calls=%fused_computation.27 | loop fusion | flops 8519680 | bytes 36700160 | tf_op jit(solution)/shard_map/cond/branch_1_fun/add | solution.py:57
  219.8 1.9 convolution_bitcast_fusion.28
  221.8 1.8 convolution_bitcast_fusion.27
  223.6 1.7 convolution_bitcast_fusion.31
  225.3 2.0 convolution_bitcast_fusion.30
  227.3 2.1 convolution_bitcast_fusion.34
  237.0 1.7 convolution_bitcast_fusion.45
  238.7 1.7 convolution_bitcast_fusion.49
  240.4 1.6 convolution_bitcast_fusion.48
  242.0 1.6 convolution_bitcast_fusion.52
  243.6 1.6 convolution_bitcast_fusion.51
  245.3 1.6 convolution_bitcast_fusion.29
  246.9 1.6 convolution_bitcast_fusion.32
  248.5 1.6 convolution_bitcast_fusion.35
  250.1 1.6 convolution_bitcast_fusion.38
  251.7 1.7 convolution_bitcast_fusion.41
  253.4 1.6 convolution_bitcast_fusion.44
  255.0 1.6 convolution_bitcast_fusion.47
  256.6 1.6 convolution_bitcast_fusion.50
  258.3 1.7 convolution_bitcast_fusion.53
  259.9 10.1 %fusion.115 = f32[320,512]{1,0:T(8,128)} fusion(f32[1,2,320,512]{3,2,1,0:T(8,128)} %get-tuple-element.36, f32[1,2,322,512]{3,2,1,0:T(8,128)S(1)} %convolution_bitcast_fusion.27, f32[1,2,322,512]{3,2,1,0:T(8,128)S(1)} %convolution_bitcast_fusion.28, f32[1,2,322,512]{3,2,1,0:T(8,128)} %convolution_bitcast_fusion.29, ...), kind=kLoop, calls=%fused_computation.198 | loop fusion | flops 9011200 | bytes 37355520 | tf_op jit(solution)/shard_map/reduce_sum | solution.py:63
  272.5 6.0 %all-reduce.3 = (f32[512]{0:T(512)S(1)}, f32[512]{0:T(512)S(1)}) all-reduce(f32[512]{0:T(512)S(1)} %get-tuple-element.18, f32[512]{0:T(512)S(1)} %get-tuple-element.17), channel_id=1, replica_groups=mesh['tm'=4,'rows'=64] {'tm'}, use_global_device_ids=true, to_apply=%region_15.16 | all-reduce | flops 1024 | bytes 8192 | tf_op jit(solution)/shard_map/psum | solution.py:12
  278.5 125.8 %all-reduce.2 = (f32[512]{0:T(512)S(1)}, f32[512]{0:T(512)S(1)}) all-reduce(f32[512]{0:T(512)S(1)} %get-tuple-element.25, f32[512]{0:T(512)S(1)} %get-tuple-element.26), channel_id=1, replica_groups=mesh['tm'=4,'rows'=64] {'rows'}, use_global_device_ids=true, to_apply=%region_16.17 | all-reduce | flops 1024 | bytes 8192 | tf_op jit(solution)/shard_map/psum | solution.py:12
  (70 shorter events, 26.3 us)
Async XLA Ops:
  7.2 23.2 %copy-start.4 = (bf16[1,2,320,512]{3,2,1,0:T(8,128)(2,1)S(1)}, bf16[1,2,320,512]{3,2,1,0:T(8,128)(2,1)}, u32[]{:S(2)}) copy-start(bf16[1,2,320,512]{3,2,1,0:T(8,128)(2,1)} %param.11) | copy-start | bytes 1966084
  7.2 164.5 %all-gather.2.cloned.1.call-start = ((), (), s32[]{:S(2)}) async-start(), calls=%async_computation | async-start | bytes 14376960 | tf_op jit(solution)/shard_map/all_gather | solution.py:95
  20.0 17.3 %copy-start.5 = (bf16[1,1,160,512]{3,2,1,0:T(8,128)(2,1)S(1)}, bf16[1,1,160,512]{3,2,1,0:T(8,128)(2,1)}, u32[]{:S(2)}) copy-start(bf16[1,1,160,512]{3,2,1,0:T(8,128)(2,1)} %param.7) | copy-start | bytes 491524
  20.1 10.2 %collective-permute-start = (bf16[1,1,320,512]{3,2,1,0:T(8,128)(2,1)S(1)}, bf16[1,1,320,512]{3,2,1,0:T(8,128)(2,1)S(1)}, u32[]{:S(2)}, u32[]{:S(2)}) collective-permute-start(bf16[1,1,320,512]{3,2,1,0:T(8,128)(2,1)S(1)} %get-tuple-element.29), channel_id=1, source_target_pairs={{0,1},{1,2},{2,3},{3,4},{4,5},{5,6},{6,7},{7,8},{8,9},{9,10},{10,1... | collective-permute-start | bytes 983048 | tf_op jit(solution)/shard_map/ppermute | solution.py:24
  26.3 8.4 %collective-permute-start.1 = (bf16[1,1,320,512]{3,2,1,0:T(8,128)(2,1)S(1)}, bf16[1,1,320,512]{3,2,1,0:T(8,128)(2,1)S(1)}, u32[]{:S(2)}, u32[]{:S(2)}) collective-permute-start(bf16[1,1,320,512]{3,2,1,0:T(8,128)(2,1)S(1)} %get-tuple-element.28), channel_id=1, source_target_pairs={{1,0},{2,1},{3,2},{4,3},{5,4},{6,5},{7,6},{8,7},{9,8},{10,9},{11,1... | collective-permute-start | bytes 983048 | tf_op jit(solution)/shard_map/ppermute | solution.py:27
  34.7 133.1 %collective-permute-start.3 = (bf16[1,4,320,512]{3,2,1,0:T(8,128)(2,1)S(1)}, bf16[1,4,320,512]{3,2,1,0:T(8,128)(2,1)}, u32[]{:S(2)}, u32[]{:S(2)}) collective-permute-start(bf16[1,4,320,512]{3,2,1,0:T(8,128)(2,1)S(1)} %constant_dynamic-update-slice_fusion), channel_id=1, source_target_pairs={{128,0},{192,64},{129,1},{193,65},{130,2},{194,66},{131,3},{195,67... | collective-permute-start | bytes 3932168 | tf_op jit(solution)/shard_map/ppermute | solution.py:35
  36.0 131.8 %collective-permute-start.2 = (bf16[1,4,320,512]{3,2,1,0:T(8,128)(2,1)S(1)}, bf16[1,4,320,512]{3,2,1,0:T(8,128)(2,1)}, u32[]{:S(2)}, u32[]{:S(2)}) collective-permute-start(bf16[1,4,320,512]{3,2,1,0:T(8,128)(2,1)S(1)} %constant_dynamic-update-slice_fusion), channel_id=1, source_target_pairs={{64,0},{128,64},{192,128},{65,1},{129,65},{193,129},{66,2},{130,66... | collective-permute-start | bytes 3932168 | tf_op jit(solution)/shard_map/ppermute | solution.py:35
  171.7 3.7 copy-start.1
  175.5 10.7 %copy-start.3 = (bf16[3,3,3,512,512]{4,3,2,1,0:T(8,128)(2,1)S(1)}, bf16[3,3,3,512,512]{4,3,2,1,0:T(8,128)(2,1)}, u32[]{:S(2)}) copy-start(bf16[3,3,3,512,512]{4,3,2,1,0:T(8,128)(2,1)} %get-tuple-element.13) | copy-start | bytes 42467332 | tf_op jit(solution)/shard_map/cond
  219.8 3.7 copy-start
  223.6 10.7 %copy-start.2 = (bf16[3,3,3,512,512]{4,3,2,1,0:T(8,128)(2,1)S(1)}, bf16[3,3,3,512,512]{4,3,2,1,0:T(8,128)(2,1)}, u32[]{:S(2)}) copy-start(bf16[3,3,3,512,512]{4,3,2,1,0:T(8,128)(2,1)} %all-gather.2.cloned.1.call-done) | copy-start | bytes 42467332
  270.0 2.3 copy-start.6
  270.0 2.3 copy-start.7
Sparse Core Ops, SparseCore 0:
  19.0 105.3 all-gather.1
